TPU v7x, 256 devices: a whole 4x4x8 slice. The times are simulated.
256 devices in a mesh: ctx: 64 (over z, x, y_hi), ch: 4 (over y_lo, core).
Axes of the slice: x: 4, y: 4 (y_hi: 2, y_lo: 2; y = y_hi * 2 + y_lo), z: 8, core: 2. Of those that a mesh axis runs over, the one named last changes fastest.
Arguments:
- query: bfloat16 [8192, 8192], P('ctx', 'ch'), may hold values from -6 to 6
- key: bfloat16 [8192, 8192], P('ctx', 'ch'), may hold values from -6 to 6
- value: bfloat16 [8192, 8192], P('ctx', 'ch'), may hold values from -6 to 6
- filter_taps: bfloat16 [1024, 512], P('ctx', 'ch'), may hold values from -0.1875 to 0.1875
- skip: float32 [8192], P('ch'), may hold values from -1 to 1
Outputs:
- gated: bfloat16 [8192, 8192], P('ctx', 'ch')
All inputs are finite; a program needn't handle non-finite values.
Results may differ from a plain program's by a relative error of at most 0.0085.
Values may be sent and summed in bfloat16 or wider, within the bound.
A program may use at most 192 MiB of HBM per device.

v0:
```python
import jax
import jax.numpy as jnp
from jax import lax
from jax.sharding import PartitionSpec as P

GROUP = 16
BLOCK = 128
LAGS = 8


def from_behind(value, axis, steps):
    count = lax.axis_size(axis)
    leading, last = (max(0, -steps), min(count, count - steps))
    return lax.ppermute(value, axis, [(source, source + steps) for source in range(leading, last)])


def all_toeplitz(padded, width, count):
    lag_part = jnp.arange(count, dtype=jnp.int32)[:, None, None] * width
    row_part = jnp.arange(width, dtype=jnp.int32)[None, :, None]
    col_part = jnp.arange(width, dtype=jnp.int32)[None, None, :]
    indices = lag_part + width + row_part - col_part
    return jnp.take(padded, indices, axis=1)


def per_device(query, key, value, filter_taps, skip):
    rows = query.shape[0]
    channels = query.shape[1]
    groups = channels // GROUP
    all_taps = lax.all_gather(filter_taps, "ctx", axis=0, tiled=True)
    mixed = (key.astype(jnp.float32) * value.astype(jnp.float32)).astype(jnp.bfloat16)
    mixed_cols = mixed.T.reshape(groups, GROUP, rows)
    padded = jnp.concatenate(
        [
            jnp.zeros((groups, BLOCK), jnp.bfloat16),
            all_taps.T,
            jnp.zeros((groups, BLOCK), jnp.bfloat16),
        ],
        axis=1,
    )
    toeplitz_all = all_toeplitz(padded, BLOCK, LAGS)

    def convolve(lag_index, source):
        return jnp.einsum(
            "gts,gcs->gct", toeplitz_all[:, lag_index], source, preferred_element_type=jnp.float32
        )

    summed = convolve(0, mixed_cols)
    moving = mixed_cols
    for lag_index in range(1, LAGS):
        moving = from_behind(moving, "ctx", 1)
        summed = summed + convolve(lag_index, moving)
    conv = summed.reshape(channels, rows).T
    gated = query.astype(jnp.float32) * (conv + skip[None, :] * mixed.astype(jnp.float32))
    return gated.astype(jnp.bfloat16)


def solution(mesh):
    placed = (P("ctx", "ch"), P("ctx", "ch"), P("ctx", "ch"), P("ctx", "ch"), P("ch"))
    return jax.shard_map(
        per_device, mesh=mesh, in_specs=placed, out_specs=P("ctx", "ch"), check_vma=False
    )
```

profile of v0, /device:TPU:128, one launch (start us, length us, event | category | flops | bytes accessed | tf_op | source)
XLA Modules:
  0.0 821.1 jit_solution(8726122279715097564)
XLA Ops:
  1.6 5.1 collective-permute-start
  7.0 15.9 %collective-permute-done = bf16[128,16,128]{2,1,0:T(8,128)(2,1)S(1)} collective-permute-done((bf16[128,16,128]{2,1,0:T(8,128)(2,1)S(1)}, bf16[128,16,128]{2,1,0:T(8,128)(2,1)S(1)}, u32[]{:S(2)}, u32[]{:S(2)}) %collective-permute-start) | collective-permute-done | bytes 524320 | tf_op jit(solution)/shard_map/ppermute | solution.py:14
  22.9 1.9 collective-permute-start.1
  24.9 18.4 %collective-permute-done.1 = bf16[128,16,128]{2,1,0:T(8,128)(2,1)S(1)} collective-permute-done((bf16[128,16,128]{2,1,0:T(8,128)(2,1)S(1)}, bf16[128,16,128]{2,1,0:T(8,128)(2,1)S(1)}, u32[]{:S(2)}, u32[]{:S(2)}) %collective-permute-start.1) | collective-permute-done | bytes 524320 | tf_op jit(solution)/shard_map/ppermute | solution.py:14
  43.3 1.9 collective-permute-start.2
  45.2 183.3 %all_gather.3 = bf16[1024,128]{1,0:T(8,128)(2,1)S(1)} all-gather(bf16[16,128]{1,0:T(8,128)(2,1)} %param.8), channel_id=1, replica_groups=mesh['ctx'=64,'ch'=4] {'ctx'}, dimensions={0}, use_global_device_ids=true | all-gather | bytes 266240 | tf_op jit(solution)/shard_map/all_gather | solution.py:29
  228.5 453.9 %gather_fusion = bf16[131072,128]{1,0:T(8,128)(2,1)} fusion(bf16[128,1280]{0,1:T(8,128)(2,1)S(1)} %pad_maximum_fusion, s32[131072]{0:T(1024)S(1)} %broadcast_clamp_fusion), kind=kCustom, calls=%fused_computation | custom fusion | bytes 67633152 | tf_op jit(solution)/shard_map/jit(_take)/gather | solution.py:22
  682.4 46.0 %copy.9 = bf16[8,128,128,128]{2,1,3,0:T(8,128)(2,1)} copy(bf16[8,128,128,128]{3,2,1,0:T(8,128)(2,1)} %bitcast.61) | data formatting | bytes 67108864 | tf_op jit(solution)/shard_map/jit(_take)/gather | solution.py:22
  728.7 5.4 collective-permute-start.3
  734.1 23.2 %select_bitcast_fusion = bf16[128,8,128,128]{3,2,0,1:T(8,128)(2,1)} fusion(bf16[8,128,128,128]{2,1,3,0:T(8,128)(2,1)} %copy.9, pred[8,128,128]{2,1,0:T(8,128)(4,1)S(1)} %fusion.19), kind=kLoop, calls=%fused_computation.1 | loop fusion | flops 16777216 | bytes 67239936 | tf_op jit(solution)/shard_map/jit(_take)/select_n | solution.py:22
  757.3 4.5 fusion.7
  761.8 1.9 collective-permute-start.4
  763.8 4.5 fusion.8
  768.3 4.5 fusion.9
  772.7 7.8 collective-permute-done.4
  780.6 1.9 collective-permute-start.5
  782.5 4.6 fusion.10
  787.1 4.7 fusion.11
  791.8 5.6 collective-permute-done.5
  799.3 4.5 fusion.12
  803.7 4.5 fusion.13
  808.2 5.9 collective-permute-done.6
  814.1 4.5 fusion.14
  819.0 2.1 fusion.16
  (23 shorter events, 4.5 us)
Async XLA Ops:
  1.6 21.3 %collective-permute-start = (bf16[128,16,128]{2,1,0:T(8,128)(2,1)S(1)}, bf16[128,16,128]{2,1,0:T(8,128)(2,1)S(1)}, u32[]{:S(2)}, u32[]{:S(2)}) collective-permute-start(bf16[128,16,128]{2,1,0:T(8,128)(2,1)S(1)} %bitcast.64), channel_id=1, source_target_pairs={{0,4},{4,8},{8,12},{12,16},{16,20},{20,24},{24,28},{28,32},{32,36}... | collective-permute-start | bytes 1572872 | tf_op jit(solution)/shard_map/ppermute | solution.py:14
  22.9 20.4 %collective-permute-start.1 = (bf16[128,16,128]{2,1,0:T(8,128)(2,1)S(1)}, bf16[128,16,128]{2,1,0:T(8,128)(2,1)S(1)}, u32[]{:S(2)}, u32[]{:S(2)}) collective-permute-start(bf16[128,16,128]{2,1,0:T(8,128)(2,1)S(1)} %collective-permute-done), channel_id=1, source_target_pairs={{0,4},{4,8},{8,12},{12,16},{16,20},{20,24},{24,28},{28,32},{32,36}... | collective-permute-start | bytes 1572872 | tf_op jit(solution)/shard_map/ppermute | solution.py:14
  43.3 639.1 %copy-start.2 = (bf16[128,16,128]{2,1,0:T(8,128)(2,1)}, bf16[128,16,128]{2,1,0:T(8,128)(2,1)S(1)}, u32[]{:S(2)}) copy-start(bf16[128,16,128]{2,1,0:T(8,128)(2,1)S(1)} %collective-permute-done.1) | copy-start | bytes 1572868
  43.3 685.4 %collective-permute-start.2 = (bf16[128,16,128]{2,1,0:T(8,128)(2,1)S(1)}, bf16[128,16,128]{2,1,0:T(8,128)(2,1)}, u32[]{:S(2)}, u32[]{:S(2)}) collective-permute-start(bf16[128,16,128]{2,1,0:T(8,128)(2,1)S(1)} %collective-permute-done.1), channel_id=1, source_target_pairs={{0,4},{4,8},{8,12},{12,16},{16,20},{20,24},{24,28},{28,32},{32,36}... | collective-permute-start | bytes 1572872 | tf_op jit(solution)/shard_map/ppermute | solution.py:14
  728.7 39.6 %copy-start.3 = (bf16[128,16,128]{2,1,0:T(8,128)(2,1)S(1)}, bf16[128,16,128]{2,1,0:T(8,128)(2,1)}, u32[]{:S(2)}) copy-start(bf16[128,16,128]{2,1,0:T(8,128)(2,1)} %copy-done.2) | copy-start | bytes 1572868
  728.7 33.2 %collective-permute-start.3 = (bf16[128,16,128]{2,1,0:T(8,128)(2,1)}, bf16[128,16,128]{2,1,0:T(8,128)(2,1)}, u32[]{:S(2)}, u32[]{:S(2)}) collective-permute-start(bf16[128,16,128]{2,1,0:T(8,128)(2,1)} %collective-permute-done.2), channel_id=1, source_target_pairs={{0,4},{4,8},{8,12},{12,16},{16,20},{20,24},{24,28},{28,32},{32,36}... | collective-permute-start | bytes 1572872 | tf_op jit(solution)/shard_map/ppermute | solution.py:14
  757.3 61.7 %copy-start = (bf16[128,2048]{1,0:T(8,128)(2,1)S(1)}, bf16[128,2048]{1,0:T(8,128)(2,1)}, u32[]{:S(2)}) copy-start(bf16[128,2048]{1,0:T(8,128)(2,1)} %param.7) | copy-start | bytes 1572868
  757.3 61.7 %copy-start.1 = (bf16[128,2048]{1,0:T(8,128)(2,1)S(1)}, bf16[128,2048]{1,0:T(8,128)(2,1)}, u32[]{:S(2)}) copy-start(bf16[128,2048]{1,0:T(8,128)(2,1)} %param.6) | copy-start | bytes 1572868
  757.3 61.7 %copy-start.4 = (f32[2048]{0:T(1024)S(1)}, f32[2048]{0:T(1024)}, u32[]{:S(2)}) copy-start(f32[2048]{0:T(1024)} %param.9) | copy-start | bytes 24580
  761.8 18.7 %collective-permute-start.4 = (bf16[128,16,128]{2,1,0:T(8,128)(2,1)}, bf16[128,16,128]{2,1,0:T(8,128)(2,1)S(1)}, u32[]{:S(2)}, u32[]{:S(2)}) collective-permute-start(bf16[128,16,128]{2,1,0:T(8,128)(2,1)} %collective-permute-done.3), channel_id=1, source_target_pairs={{0,4},{4,8},{8,12},{12,16},{16,20},{20,24},{24,28},{28,32},{32,36}... | collective-permute-start | bytes 1572872 | tf_op jit(solution)/shard_map/ppermute | solution.py:14
  780.6 16.8 %collective-permute-start.5 = (bf16[128,16,128]{2,1,0:T(8,128)(2,1)S(1)}, bf16[128,16,128]{2,1,0:T(8,128)(2,1)S(1)}, u32[]{:S(2)}, u32[]{:S(2)}) collective-permute-start(bf16[128,16,128]{2,1,0:T(8,128)(2,1)S(1)} %collective-permute-done.4), channel_id=1, source_target_pairs={{0,4},{4,8},{8,12},{12,16},{16,20},{20,24},{24,28},{28,32},{32,36}... | collective-permute-start | bytes 1572872 | tf_op jit(solution)/shard_map/ppermute | solution.py:14
  797.4 16.8 %collective-permute-start.6 = (bf16[128,16,128]{2,1,0:T(8,128)(2,1)S(1)}, bf16[128,16,128]{2,1,0:T(8,128)(2,1)S(1)}, u32[]{:S(2)}, u32[]{:S(2)}) collective-permute-start(bf16[128,16,128]{2,1,0:T(8,128)(2,1)S(1)} %collective-permute-done.5), channel_id=1, source_target_pairs={{0,4},{4,8},{8,12},{12,16},{16,20},{20,24},{24,28},{28,32},{32,36}... | collective-permute-start | bytes 1572872 | tf_op jit(solution)/shard_map/ppermute | solution.py:14
where the time goes:
time: 823 us; the launch traced here: 821 us
  local copies, waits for them, and re-layouts  501 us (61%)
  blocking collectives  183 us (22%)
  waiting for transfers between devices  53.6 us (7%)
  matrix products  36.2 us (4%)
  other arithmetic  27.2 us (3%)
  starting transfers between devices  20.1 us (2%)
    gather x2, local copies, waits for them, and re-layouts, all_toeplitz(): return jnp.take(padded, indices, axis=1)  500 us
    all_gather x1, blocking collectives, per_device(): all_taps = lax.all_gather(filter_taps, 'ctx', axis=0, tiled=True)  183 us
    ppermute x7, waiting for transfers between devices, from_behind(): lax.ppermute(value, axis, [(source, source + steps) for source in range(l...  53.6 us
    dot_general x8, matrix products, convolve(): jnp.einsum('gts,gcs->gct', toeplitz_all[:, lag_index], source, preferred_...  36.2 us
    select_n x2, other arithmetic, all_toeplitz(): return jnp.take(padded, indices, axis=1)  23.4 us
    ppermute x7, starting transfers between devices, from_behind(): lax.ppermute(value, axis, [(source, source + steps) for source in range(l...  20.1 us
  transfers between devices with their start and end apart: 7, of which 5 were waited for; matrix products, arithmetic and copies ran while one was open for 68% of the time, Pallas kernels for 0%

commit v1 on v0

v1 whole, which is shorter than its diff:
```python
import functools

import jax
import jax.numpy as jnp
from jax import lax
from jax.experimental import pallas as pl
from jax.experimental.pallas import tpu as pltpu
from jax.sharding import PartitionSpec as P

MESH = pl.DeviceIdType.MESH
GROUP = 16
BLOCK = 128
LAGS = 8
PLANE = 8
CHUNKS = 2


def kernel(planes, q_hbm, k_hbm, v_hbm, taps_hbm, skip_hbm, out_ref,
           q_v, k_v, v_v, skip_v, skip_rows, mixed, source, taps_in, taps_f, taps_own, taps_all, taps_row,
           toeplitz, result, back,
           load_sem, tap_send, tap_recv, line_send, line_recv, credit,
           own_send, own_recv, halo_send, halo_recv, back_send, back_recv):
    ctx, ch = lax.axis_index("ctx"), lax.axis_index("ch")
    z, me = ctx // PLANE, ctx % PLANE
    last = planes - 1
    groups = source.shape[0]
    part = groups // CHUNKS

    def at(plane, place):
        return (plane * PLANE + place, ch)

    def remote(src, dst, send, recv, device):
        return pltpu.make_async_remote_copy(
            src_ref=src, dst_ref=dst, send_sem=send, recv_sem=recv,
            device_id=device, device_id_type=MESH)

    barrier = pltpu.get_barrier_semaphore()
    for step in range(1, PLANE):
        pl.semaphore_signal(barrier, inc=1, device_id=at(z, (me + step) % PLANE), device_id_type=MESH)

    @pl.when(z > 0)
    def _():
        for step in range(PLANE):
            pl.semaphore_signal(barrier, inc=1, device_id=at(z - 1, (me + step) % PLANE), device_id_type=MESH)

    for step in range(1, planes):
        @pl.when(z + step < planes)
        def _(step=step):
            pl.semaphore_signal(barrier, inc=1, device_id=at(z + step, me), device_id_type=MESH)

    loads = [
        pltpu.make_async_copy(k_hbm, k_v, load_sem.at[0]),
        pltpu.make_async_copy(v_hbm, v_v, load_sem.at[1]),
        pltpu.make_async_copy(taps_hbm, taps_in.at[me], load_sem.at[2]),
        pltpu.make_async_copy(skip_hbm.at[pl.ds(pl.multiple_of(me * groups * GROUP, 256), groups * GROUP)], skip_v, load_sem.at[3]),
        pltpu.make_async_copy(q_hbm, q_v, load_sem.at[4]),
    ]
    for load in loads:
        load.start()

    @pl.when(z == 0)
    def _():
        source[:, 0:LAGS - 1] = jnp.zeros((groups, LAGS - 1, GROUP, BLOCK), jnp.bfloat16)

    pl.semaphore_wait(barrier, PLANE - 1 + z + jnp.where(z < last, PLANE, 0))

    tap_copies = []
    for step in range(1, PLANE):
        copy = remote(taps_hbm, taps_in.at[me], tap_send, tap_recv, at(z, (me + step) % PLANE))
        copy.start()
        tap_copies.append(copy)

    loads[0].wait()
    loads[1].wait()
    own_copies = []
    local_copies = []
    halo_copies = []
    for chunk in range(CHUNKS):
        rows = pl.ds(chunk * part, part)
        for step in range(1, PLANE + 1):
            to = (me + step) % PLANE
            width = part * GROUP
            lanes = pl.ds(pl.multiple_of(to * groups * GROUP + chunk * width, width), width)
            m = (k_v[:, lanes].astype(jnp.float32) * v_v[:, lanes].astype(jnp.float32))
            m = m.T.astype(jnp.bfloat16).reshape(part, GROUP, BLOCK)
            mixed[to, rows] = m
            if step < PLANE:
                copy = remote(mixed.at[to, rows], source.at[rows, LAGS - 1 + me], own_send, own_recv.at[chunk], at(z, to))
                copy.start()
                own_copies.append(copy)
            else:
                copy = pltpu.make_async_copy(mixed.at[to, rows], source.at[rows, LAGS - 1 + me], load_sem.at[5 + chunk])
                copy.start()
                local_copies.append(copy)

            @pl.when((z < last) & (me > 0))
            def _(to=to, rows=rows, chunk=chunk):
                remote(mixed.at[to, rows], source.at[rows, jnp.maximum(me - 1, 0)], halo_send, halo_recv.at[chunk],
                       at(jnp.minimum(z + 1, last), to)).start()

    loads[2].wait()
    pltpu.make_async_copy(taps_in.at[0:PLANE - 1], taps_in.at[0:PLANE - 1], tap_recv).wait()
    taps_f[...] = taps_in[...].astype(jnp.float32).reshape(BLOCK, BLOCK).T
    taps_own[...] = taps_f[pl.ds(pl.multiple_of(me * groups, groups), groups), :].astype(jnp.bfloat16)

    def line(step):
        return remote(taps_own, taps_all.at[z], line_send, line_recv, at(jnp.clip(z + step, 0, last), me))

    for step in range(-last, 2):
        if step != 0:
            @pl.when((z + step >= 0) & (z + step <= last))
            def _(step=step):
                line(step).start()
    for step in range(2, planes):
        @pl.when(z - step >= 0)
        def _(step=step):
            pl.semaphore_signal(credit, inc=1, device_id=at(z - step, me), device_id_type=MESH)

    @pl.when(z < last - 1)
    def _():
        pl.semaphore_wait(credit, last - 1 - z)

    for step in range(2, planes):
        @pl.when(z + step <= last)
        def _(step=step):
            line(step).start()
    taps_all[z] = taps_own[...]

    pltpu.make_async_copy(taps_all.at[0:planes - 1], taps_all.at[0:planes - 1], line_recv).wait()

    taps_row[...] = taps_all[...].astype(jnp.float32)
    u = lax.broadcasted_iota(jnp.int32, (BLOCK, BLOCK), 0)
    t = lax.broadcasted_iota(jnp.int32, (BLOCK, BLOCK), 1)
    reached = t >= u

    @pl.loop(0, groups)
    def _(g):
        before = jnp.zeros((BLOCK, BLOCK), jnp.float32)
        for lag in range(LAGS):
            row = taps_row[lag, pl.ds(g, 1), :]
            turned = pltpu.roll(jnp.broadcast_to(row, (BLOCK, BLOCK)), 0, 1, stride=1, stride_axis=0)
            toeplitz[g, lag * BLOCK:(lag + 1) * BLOCK, :] = jnp.where(reached, turned, before).astype(jnp.bfloat16)
            before = turned

    loads[3].wait()
    for half in range(groups * GROUP // BLOCK):
        row = skip_v[half * BLOCK:(half + 1) * BLOCK].reshape(1, BLOCK)
        per = BLOCK // GROUP
        skip_rows[half * per:(half + 1) * per] = jnp.broadcast_to(row, (BLOCK, BLOCK)).T.reshape(per, GROUP, BLOCK)

    for copy in local_copies:
        copy.wait()
    back_copies = []
    for chunk in range(CHUNKS):
        rows = pl.ds(chunk * part, part)
        landed = mixed.at[0:PLANE - 1, rows]
        pltpu.make_async_copy(landed, landed, own_recv.at[chunk]).wait()

        @pl.when(z > 0)
        def _(landed=landed, chunk=chunk):
            pltpu.make_async_copy(landed, landed, halo_recv.at[chunk]).wait()

        @pl.loop(chunk * part, (chunk + 1) * part)
        def _(g):
            total = jnp.broadcast_to(skip_rows[g][None], (PLANE, GROUP, BLOCK)).reshape(BLOCK, BLOCK)
            total = total * source[g, LAGS - 1:LAGS - 1 + PLANE].reshape(BLOCK, BLOCK).astype(jnp.float32)
            for lag in range(0, LAGS, 2):
                here = source[g, LAGS - 1 - lag:LAGS - 1 - lag + PLANE].reshape(BLOCK, BLOCK)
                there = source[g, LAGS - 2 - lag:LAGS - 2 - lag + PLANE].reshape(BLOCK, BLOCK)
                total = total + jnp.dot(
                    jnp.concatenate([here, there], axis=1),
                    toeplitz[g, lag * BLOCK:(lag + 2) * BLOCK, :],
                    preferred_element_type=jnp.float32)
            result[:, g] = total.astype(jnp.bfloat16).reshape(PLANE, GROUP, BLOCK)

        for step in range(1, PLANE + 1):
            to = (me + step) % PLANE
            if step < PLANE:
                copy = remote(result.at[to, rows], back.at[me, rows], back_send, back_recv.at[chunk], at(z, to))
                copy.start()
                back_copies.append(copy)
            else:
                back[me, rows] = result[me, rows]

    loads[4].wait()
    for chunk in range(CHUNKS):
        rows = pl.ds(chunk * part, part)
        landed = mixed.at[0:PLANE - 1, rows]
        pltpu.make_async_copy(landed, landed, back_recv.at[chunk]).wait()
        for place in range(PLANE):
            width = part * GROUP
            first = place * groups * GROUP + chunk * width
            lanes = slice(first, first + width)
            turned = back[place, rows].reshape(width, BLOCK).astype(jnp.float32).T
            out_ref[:, lanes] = (q_v[:, lanes].astype(jnp.float32) * turned).astype(jnp.bfloat16)

    for copy in tap_copies + own_copies + back_copies:
        copy.wait_send()
    for step in range(1, planes):
        line(1).wait_send()

    @pl.when((z < last) & (me > 0))
    def _():
        for chunk in range(CHUNKS):
            rows = pl.ds(chunk * part, part)
            for _ in range(PLANE):
                remote(mixed.at[0, rows], source.at[rows, 0], halo_send, halo_recv.at[chunk], at(z, me)).wait_send()


def solution(mesh):
    planes = mesh.shape["ctx"] // PLANE

    def per_device(query, key, value, filter_taps, skip):
        tokens, channels = query.shape
        groups = channels // GROUP // PLANE
        hbm = pl.BlockSpec(memory_space=pl.ANY)
        bf16, f32 = jnp.bfloat16, jnp.float32
        dma = pltpu.SemaphoreType.DMA
        return pl.pallas_call(
            functools.partial(kernel, planes),
            out_shape=jax.ShapeDtypeStruct((tokens, channels), bf16),
            in_specs=[hbm] * 5,
            out_specs=pl.BlockSpec(memory_space=pltpu.VMEM),
            scratch_shapes=[
                pltpu.VMEM((tokens, channels), bf16),
                pltpu.VMEM((tokens, channels), bf16),
                pltpu.VMEM((tokens, channels), bf16),
                pltpu.VMEM((groups * GROUP,), f32),
                pltpu.VMEM((groups, GROUP, BLOCK), f32),
                pltpu.VMEM((PLANE, groups, GROUP, BLOCK), bf16),
                pltpu.VMEM((groups, LAGS - 1 + PLANE, GROUP, BLOCK), bf16),
                pltpu.VMEM((PLANE, BLOCK // PLANE, BLOCK), bf16),
                pltpu.VMEM((BLOCK, BLOCK), f32),
                pltpu.VMEM((groups, BLOCK), bf16),
                pltpu.VMEM((planes, groups, BLOCK), bf16),
                pltpu.VMEM((planes, groups, BLOCK), f32),
                pltpu.VMEM((groups, LAGS * BLOCK, BLOCK), bf16),
                pltpu.VMEM((PLANE, groups, GROUP, BLOCK), bf16),
                pltpu.VMEM((PLANE, groups, GROUP, BLOCK), bf16),
                dma((5 + CHUNKS,)),
                dma, dma, dma, dma,
                pltpu.SemaphoreType.REGULAR,
                dma, dma((CHUNKS,)), dma, dma((CHUNKS,)), dma, dma((CHUNKS,)),
            ],
            compiler_params=pltpu.CompilerParams(collective_id=0, has_side_effects=True, vmem_limit_bytes=48 << 20),
        )(query, key, value, filter_taps, skip)

    placed = (P("ctx", "ch"), P("ctx", "ch"), P("ctx", "ch"), P("ctx", "ch"), P("ch"))
    return jax.shard_map(per_device, mesh=mesh, in_specs=placed, out_specs=P("ctx", "ch"), check_vma=False)
```

time: 823 us -> 41.7 us (0.05)
  the two profiles are of different devices: /device:TPU:128 before, /device:TPU:8 now
where the time goes in v1:
time: 41.7 us; the launch traced here: 41.2 us
  Pallas kernels  35.9 us (86%)
  local copies, waits for them, and re-layouts  5.3 us (13%)
    pallas_call x1, Pallas kernels, per_device(): pl.pallas_call(functools.partial(kernel, planes), out_shape=jax.ShapeDtyp...  35.9 us
    unnamed x11, local copies, waits for them, and re-layouts  5.3 us

profile of v1, /device:TPU:8, one launch (start us, length us, event | category | flops | bytes accessed | tf_op | source)
XLA Modules:
  0.0 41.2 jit_solution(8159183471812089073)
XLA Ops:
  0.0 0.0 copy-start
  0.0 1.0 %copy-done = bf16[128,2048]{1,0:T(8,128)(2,1)S(1)} copy-done((bf16[128,2048]{1,0:T(8,128)(2,1)S(1)}, bf16[128,2048]{1,0:T(8,128)(2,1)}, u32[]{:S(2)}) %copy-start) | copy-done | bytes 524312
  1.0 0.0 copy-start.1
  1.0 1.0 %copy-done.1 = bf16[128,2048]{1,0:T(8,128)(2,1)S(1)} copy-done((bf16[128,2048]{1,0:T(8,128)(2,1)S(1)}, bf16[128,2048]{1,0:T(8,128)(2,1)}, u32[]{:S(2)}) %copy-start.1) | copy-done | bytes 524312
  2.1 0.0 copy-start.2
  2.1 1.0 %copy-done.2 = bf16[128,2048]{1,0:T(8,128)(2,1)S(1)} copy-done((bf16[128,2048]{1,0:T(8,128)(2,1)S(1)}, bf16[128,2048]{1,0:T(8,128)(2,1)}, u32[]{:S(2)}) %copy-start.2) | copy-done | bytes 524312
  3.1 0.0 copy-start.3
  3.1 0.7 %copy-done.3 = f32[2048]{0:T(1024)S(1)} copy-done((f32[2048]{0:T(1024)S(1)}, f32[2048]{0:T(1024)}, u32[]{:S(2)}) %copy-start.3) | copy-done | bytes 8216
  3.8 0.0 copy-start.4
  3.8 0.7 %copy-done.4 = bf16[16,128]{1,0:T(8,128)(2,1)S(1)} copy-done((bf16[16,128]{1,0:T(8,128)(2,1)S(1)}, bf16[16,128]{1,0:T(8,128)(2,1)}, u32[]{:S(2)}) %copy-start.4) | copy-done | bytes 4120
  4.5 35.9 %shard_map.55 = bf16[128,2048]{1,0:T(8,128)(2,1)S(1)} custom-call(bf16[128,2048]{1,0:T(8,128)(2,1)S(1)} %copy-done, bf16[128,2048]{1,0:T(8,128)(2,1)S(1)} %copy-done.1, bf16[128,2048]{1,0:T(8,128)(2,1)S(1)} %copy-done.2, bf16[16,128]{1,0:T(8,128)(2,1)S(1)} %copy-done.4, f32[2048]{0:T(1024)S(1)} %copy-done.3), custom_call_target="tpu_custom_call" | custom-call | tf_op jit(solution)/shard_map/pallas_call | solution.py:219
  40.4 0.8 %copy.7 = bf16[128,2048]{1,0:T(8,128)(2,1)} copy(bf16[128,2048]{1,0:T(8,128)(2,1)S(1)} %shard_map.55) | data formatting | bytes 1048576
Async XLA Ops:
  0.0 1.0 %copy-start = (bf16[128,2048]{1,0:T(8,128)(2,1)S(1)}, bf16[128,2048]{1,0:T(8,128)(2,1)}, u32[]{:S(2)}) copy-start(bf16[128,2048]{1,0:T(8,128)(2,1)} %q_hbm.1) | copy-start | bytes 1572868
  1.0 1.0 %copy-start.1 = (bf16[128,2048]{1,0:T(8,128)(2,1)S(1)}, bf16[128,2048]{1,0:T(8,128)(2,1)}, u32[]{:S(2)}) copy-start(bf16[128,2048]{1,0:T(8,128)(2,1)} %k_hbm.1) | copy-start | bytes 1572868
  2.1 1.0 %copy-start.2 = (bf16[128,2048]{1,0:T(8,128)(2,1)S(1)}, bf16[128,2048]{1,0:T(8,128)(2,1)}, u32[]{:S(2)}) copy-start(bf16[128,2048]{1,0:T(8,128)(2,1)} %v_hbm.1) | copy-start | bytes 1572868
  3.1 0.7 %copy-start.3 = (f32[2048]{0:T(1024)S(1)}, f32[2048]{0:T(1024)}, u32[]{:S(2)}) copy-start(f32[2048]{0:T(1024)} %skip_hbm.1) | copy-start | bytes 24580
  3.8 0.7 %copy-start.4 = (bf16[16,128]{1,0:T(8,128)(2,1)S(1)}, bf16[16,128]{1,0:T(8,128)(2,1)}, u32[]{:S(2)}) copy-start(bf16[16,128]{1,0:T(8,128)(2,1)} %taps_hbm.1) | copy-start | bytes 12292

commit v2 on v1

v2 whole, which is shorter than its diff:
```python
import functools

import jax
import jax.numpy as jnp
from jax import lax
from jax.experimental import pallas as pl
from jax.experimental.pallas import tpu as pltpu
from jax.sharding import PartitionSpec as P

MESH = pl.DeviceIdType.MESH
GROUP = 16
BLOCK = 128
LAGS = 8
PLANE = 8
ORDER = (0, 1)
DIRECT = (0, 1)
STEPS = 2
CHUNKS = 4


def kernel(planes, k_hbm, v_hbm, taps_hbm, skip_hbm, back,
           k_v, v_v, skip_v, skip_rows, mixed, source, taps_in, taps_f, taps_own, taps_all, taps_row,
           toeplitz, result,
           load_sem, local_sem, tap_send, tap_recv, line_send, line_recv, credit,
           own_send, own_recv, halo_send, halo_recv, back_send, back_recv):
    ctx, ch = lax.axis_index("ctx"), lax.axis_index("ch")
    z, me = ctx // PLANE, ctx % PLANE
    last = planes - 1
    groups = source.shape[0]
    half = groups // 2
    width = half * GROUP
    part = groups // CHUNKS
    f32, bf16 = jnp.float32, jnp.bfloat16

    def at(plane, place):
        return (plane * PLANE + place, ch)

    def remote(src, dst, send, recv, device):
        return pltpu.make_async_remote_copy(
            src_ref=src, dst_ref=dst, send_sem=send, recv_sem=recv,
            device_id=device, device_id_type=MESH)

    barrier = pltpu.get_barrier_semaphore()
    for step in range(1, PLANE):
        pl.semaphore_signal(barrier, inc=1, device_id=at(z, (me + step) % PLANE), device_id_type=MESH)

    @pl.when(z > 0)
    def _():
        for step in range(PLANE):
            pl.semaphore_signal(barrier, inc=1, device_id=at(z - 1, (me + step) % PLANE), device_id_type=MESH)

    for step in range(1, planes):
        @pl.when(z + step < planes)
        def _(step=step):
            pl.semaphore_signal(barrier, inc=1, device_id=at(z + step, me), device_id_type=MESH)

    loads = [
        pltpu.make_async_copy(k_hbm, k_v, load_sem.at[0]),
        pltpu.make_async_copy(v_hbm, v_v, load_sem.at[1]),
        pltpu.make_async_copy(taps_hbm, taps_in.at[me], load_sem.at[2]),
        pltpu.make_async_copy(skip_hbm.at[pl.ds(pl.multiple_of(me * groups * GROUP, 256), groups * GROUP)], skip_v, load_sem.at[3]),
    ]
    for load in loads:
        load.start()

    @pl.when(z == 0)
    def _():
        source[:, 0:LAGS - 1] = jnp.zeros((groups, LAGS - 1, GROUP, BLOCK), bf16)

    pl.semaphore_wait(barrier, PLANE - 1 + z + jnp.where(z < last, PLANE, 0))

    tap_copies = []
    for step in range(1, PLANE):
        copy = remote(taps_hbm, taps_in.at[me], tap_send, tap_recv, at(z, (me + step) % PLANE))
        copy.start()
        tap_copies.append(copy)

    for step in range(2, planes):
        @pl.when(z - step >= 0)
        def _(step=step):
            pl.semaphore_signal(credit, inc=1, device_id=at(z - step, me), device_id_type=MESH)

    loads[0].wait()
    loads[1].wait()
    own_copies = []
    local_copies = {}

    def halves(which):
        return pl.ds(which * half, half)

    def mix(to, which):
        lanes = pl.ds(pl.multiple_of(to * groups * GROUP + which * width, width), width)
        m = (k_v[:, lanes].astype(f32) * v_v[:, lanes].astype(f32)).T
        mixed[to, halves(which)] = m.astype(bf16).reshape(half, GROUP, BLOCK)

    def send_own(to, which):
        copy = remote(mixed.at[to, halves(which)], source.at[halves(which), LAGS - 1 + me], own_send, own_recv.at[which], at(z, to))
        copy.start()
        own_copies.append(copy)

    def keep_own(which):
        copy = pltpu.make_async_copy(mixed.at[me, halves(which)], source.at[halves(which), LAGS - 1 + me], local_sem.at[which])
        copy.start()
        local_copies[which] = copy

    def halo(to, which):
        return remote(mixed.at[to, halves(which)], source.at[halves(which), jnp.maximum(me - 1, 0)], halo_send.at[0], halo_recv.at[which],
                      at(jnp.minimum(z + 1, last), to))

    def forward(which):
        return remote(source.at[halves(which), LAGS:LAGS + PLANE - 1], source.at[halves(which), 0:LAGS - 1], halo_send.at[1],
                      halo_recv.at[which], at(jnp.minimum(z + 1, last), me))

    places = [(me + step) % PLANE for step in range(1, PLANE)] + [me]
    for which in ORDER:
        for to in places:
            mix(to, which)
            if to is not me:
                send_own(to, which)
            if which in DIRECT:
                @pl.when((z < last) & (me > 0))
                def _(to=to, which=which):
                    halo(to, which).start()
        keep_own(which)

    loads[2].wait()
    pltpu.make_async_copy(taps_in.at[0:PLANE - 1], taps_in.at[0:PLANE - 1], tap_recv).wait()
    taps_f[...] = taps_in[...].astype(f32).reshape(BLOCK, BLOCK).T
    taps_own[...] = taps_f[pl.ds(pl.multiple_of(me * groups, groups), groups), :].astype(bf16)

    def line(step):
        return remote(taps_own, taps_all.at[z], line_send, line_recv.at[z], at(jnp.clip(z + step, 0, last), me))

    for step in range(-last, 2):
        if step != 0:
            @pl.when((z + step >= 0) & (z + step <= last))
            def _(step=step):
                line(step).start()
    taps_all[z] = taps_own[...]

    loads[3].wait()
    per = BLOCK // GROUP
    for piece in range(groups // per):
        row = skip_v[piece * BLOCK:(piece + 1) * BLOCK].reshape(1, BLOCK)
        skip_rows[piece * per:(piece + 1) * per] = jnp.broadcast_to(row, (BLOCK, BLOCK)).T.reshape(per, GROUP, BLOCK)

    landed = mixed.at[0:PLANE - 1, pl.ds(0, half)]

    def wait_own(which):
        local_copies[which].wait()
        pltpu.make_async_copy(landed, landed, own_recv.at[which]).wait()

    for which in ORDER:
        if which not in DIRECT:
            wait_own(which)

            @pl.when(z < last)
            def _(which=which):
                forward(which).start()

    @pl.when(z < last - 1)
    def _():
        pl.semaphore_wait(credit, last - 1 - z)

    for step in range(2, planes):
        @pl.when(z + step <= last)
        def _(step=step):
            line(step).start()

    u = lax.broadcasted_iota(jnp.int32, (BLOCK, BLOCK), 0)
    t = lax.broadcasted_iota(jnp.int32, (BLOCK, BLOCK), 1)
    reached = t >= u

    def turn(lag, g):
        row = taps_row[lag, pl.ds(g, 1), :]
        return pltpu.roll(jnp.broadcast_to(row, (BLOCK, BLOCK)), 0, 1, stride=1, stride_axis=0)

    def rows_of(lags):
        for lag in lags:
            @pl.when(z != lag)
            def _(lag=lag):
                pltpu.make_async_copy(taps_own, taps_own, line_recv.at[lag]).wait()
            taps_row[lag] = taps_all[lag].astype(f32)

    def build(lags, g):
        before = turn(lags[0] - 1, g) if lags[0] else jnp.zeros((BLOCK, BLOCK), f32)
        for lag in lags:
            turned = turn(lag, g)
            toeplitz[g, lag * BLOCK:(lag + 1) * BLOCK, :] = jnp.where(reached, turned, before).astype(bf16)
            before = turned

    early, late = range(0, LAGS // 2), range(LAGS // 2, LAGS)
    rows_of(early)

    @pl.loop(0, groups, unroll=2)
    def _(g):
        build(early, g)

    rows_of(late)

    back_copies = []
    for chunk in range(CHUNKS):
        rows = pl.ds(chunk * part, part)
        which = chunk * part // half
        if chunk * part % half == 0:
            if which in DIRECT:
                wait_own(which)

            @pl.when(z > 0)
            def _(which=which):
                pltpu.make_async_copy(landed, landed, halo_recv.at[which]).wait()

        @pl.loop(chunk * part, (chunk + 1) * part, unroll=part)
        def _(g):
            build(late, g)
            total = jnp.broadcast_to(skip_rows[g][None], (PLANE, GROUP, BLOCK)).reshape(BLOCK, BLOCK)
            total = total * source[g, LAGS - 1:LAGS - 1 + PLANE].reshape(BLOCK, BLOCK).astype(f32)
            windows = [source[g, LAGS - 1 - lag:LAGS - 1 - lag + PLANE].reshape(BLOCK, BLOCK) for lag in range(LAGS)]
            total = total + jnp.dot(jnp.concatenate(windows, axis=1), toeplitz[g], preferred_element_type=f32)
            result[:, g] = total.astype(bf16).reshape(PLANE, GROUP, BLOCK)

        for to in places[:-1]:
            copy = remote(result.at[to, rows], back.at[me, rows], back_send, back_recv, at(z, to))
            copy.start()
            back_copies.append(copy)
    home = pltpu.make_async_copy(result.at[me], back.at[me], local_sem.at[2])
    home.start()
    home.wait()

    for copy in tap_copies + own_copies + back_copies:
        copy.wait_send()
    for step in range(1, planes):
        line(1).wait_send()

    @pl.when((z < last) & (me > 0))
    def _():
        for which in DIRECT:
            for _ in range(PLANE):
                halo(me, which).wait_send()

    @pl.when(z < last)
    def _():
        for which in range(2):
            if which not in DIRECT:
                forward(which).wait_send()

    pltpu.make_async_copy(back.at[0:PLANE - 1], back.at[0:PLANE - 1], back_recv).wait()


def gate(back_ref, q_ref, out_ref):
    for first in range(0, q_ref.shape[1], BLOCK):
        lanes = slice(first, first + BLOCK)
        turned = back_ref[lanes, :].astype(jnp.float32).T
        out_ref[:, lanes] = (q_ref[:, lanes].astype(jnp.float32) * turned).astype(jnp.bfloat16)


def solution(mesh):
    planes = mesh.shape["ctx"] // PLANE

    def per_device(query, key, value, filter_taps, skip):
        tokens, channels = query.shape
        groups = channels // GROUP // PLANE
        hbm = pl.BlockSpec(memory_space=pl.ANY)
        bf16, f32 = jnp.bfloat16, jnp.float32
        dma = pltpu.SemaphoreType.DMA
        back = pl.pallas_call(
            functools.partial(kernel, planes),
            out_shape=jax.ShapeDtypeStruct((PLANE, groups, GROUP, BLOCK), bf16),
            in_specs=[hbm] * 4,
            out_specs=hbm,
            scratch_shapes=[
                pltpu.VMEM((tokens, channels), bf16),
                pltpu.VMEM((tokens, channels), bf16),
                pltpu.VMEM((groups * GROUP,), f32),
                pltpu.VMEM((groups, GROUP, BLOCK), f32),
                pltpu.VMEM((PLANE, groups, GROUP, BLOCK), bf16),
                pltpu.VMEM((groups, LAGS - 1 + PLANE, GROUP, BLOCK), bf16),
                pltpu.VMEM((PLANE, BLOCK // PLANE, BLOCK), bf16),
                pltpu.VMEM((BLOCK, BLOCK), f32),
                pltpu.VMEM((groups, BLOCK), bf16),
                pltpu.VMEM((planes, groups, BLOCK), bf16),
                pltpu.VMEM((planes, groups, BLOCK), f32),
                pltpu.VMEM((groups, LAGS * BLOCK, BLOCK), bf16),
                pltpu.VMEM((PLANE, groups, GROUP, BLOCK), bf16),
                dma((4,)), dma((3,)),
                dma, dma, dma, dma((planes,)),
                pltpu.SemaphoreType.REGULAR,
                dma, dma((2,)), dma((2,)), dma((2,)), dma, dma,
            ],
            compiler_params=pltpu.CompilerParams(collective_id=0, has_side_effects=True),
        )(key, value, filter_taps, skip)
        steps = STEPS
        return pl.pallas_call(
            gate,
            grid=(steps,),
            out_shape=jax.ShapeDtypeStruct((tokens, channels), bf16),
            in_specs=[pl.BlockSpec((channels // steps, BLOCK), lambda i: (i, 0)), pl.BlockSpec((tokens, channels // steps), lambda i: (0, i))],
            out_specs=pl.BlockSpec((tokens, channels // steps), lambda i: (0, i)),
        )(back.reshape(channels, BLOCK), query)

    placed = (P("ctx", "ch"), P("ctx", "ch"), P("ctx", "ch"), P("ctx", "ch"), P("ch"))
    return jax.shard_map(per_device, mesh=mesh, in_specs=placed, out_specs=P("ctx", "ch"), check_vma=False)
```

time: 41.7 us -> 34.3 us (0.82)
  local copies, waits for them, and re-layouts: 5.3 us -> 0 us
  Pallas kernels: 35.9 us -> 34.2 us
    unnamed x11 -> x0, local copies, waits for them, and re-layouts: 5.3 us -> none
    pallas_call x1, Pallas kernels: 35.9 us -> 32.1 us  [per_device(): pl.pallas_call(functools.partial(kernel, planes), out_shape=jax.ShapeDtyp...]
    pallas_call x0 -> x1, Pallas kernels: none -> 2.05 us  [per_device(): pl.pallas_call(gate, grid=(steps,), out_shape=jax.ShapeDtypeStruct((token...]
where the time goes in v2:
time: 34.3 us; the launch traced here: 34.2 us
  Pallas kernels  34.2 us (100%)
    pallas_call x1, Pallas kernels, per_device(): pl.pallas_call(functools.partial(kernel, planes), out_shape=jax.ShapeDtyp...  32.1 us
    pallas_call x1, Pallas kernels, per_device(): pl.pallas_call(gate, grid=(steps,), out_shape=jax.ShapeDtypeStruct((token...  2.05 us

profile of v2, /device:TPU:8, one launch (start us, length us, event | category | flops | bytes accessed | tf_op | source)
XLA Modules:
  0.0 34.2 jit_solution(5528404688069782978)
XLA Ops:
  0.0 32.1 %shard_map.55 = bf16[8,16,16,128]{3,2,1,0:T(8,128)(2,1)} custom-call(bf16[128,2048]{1,0:T(8,128)(2,1)} %k_hbm.1, bf16[128,2048]{1,0:T(8,128)(2,1)} %v_hbm.1, bf16[16,128]{1,0:T(8,128)(2,1)} %taps_hbm.1, f32[2048]{0:T(1024)} %skip_hbm.1), custom_call_target="tpu_custom_call" | custom-call | tf_op jit(solution)/shard_map/pallas_call | solution.py:266
  32.1 2.0 %shard_map.56 = bf16[128,2048]{1,0:T(8,128)(2,1)} custom-call(bf16[2048,128]{1,0:T(8,128)(2,1)} %bitcast.1, bf16[128,2048]{1,0:T(8,128)(2,1)} %q_ref.1), custom_call_target="tpu_custom_call" | custom-call | tf_op jit(solution)/shard_map/pallas_call | solution.py:293

commit v3 on v2

--- a/solution.py
+++ b/solution.py
@@ -12,8 +12,7 @@
 BLOCK = 128
 LAGS = 8
 PLANE = 8
-ORDER = (0, 1)
-DIRECT = (0, 1)
+PLAN = ((('m', 0), ('m', 1), ('o', 3), ('o', 0), ('h', 0), ('h', 1)), (('h', 2), ('o', 1), ('o', 2)), (('f', 3),), ())
 STEPS = 2
 CHUNKS = 4
 
@@ -84,44 +83,64 @@
     loads[1].wait()
     own_copies = []
     local_copies = {}
-
-    def halves(which):
-        return pl.ds(which * half, half)
+    pieces = [pl.ds(chunk * part, part) for chunk in range(CHUNKS)]
 
     def mix(to, which):
         lanes = pl.ds(pl.multiple_of(to * groups * GROUP + which * width, width), width)
         m = (k_v[:, lanes].astype(f32) * v_v[:, lanes].astype(f32)).T
-        mixed[to, halves(which)] = m.astype(bf16).reshape(half, GROUP, BLOCK)
-
-    def send_own(to, which):
-        copy = remote(mixed.at[to, halves(which)], source.at[halves(which), LAGS - 1 + me], own_send, own_recv.at[which], at(z, to))
+        mixed[to, pl.ds(which * half, half)] = m.astype(bf16).reshape(half, GROUP, BLOCK)
+
+    def send_own(chunk):
+        for to in places[:-1]:
+            copy = remote(mixed.at[to, pieces[chunk]], source.at[pieces[chunk], LAGS - 1 + me], own_send, own_recv.at[chunk], at(z, to))
+            copy.start()
+            own_copies.append(copy)
+        copy = pltpu.make_async_copy(mixed.at[me, pieces[chunk]], source.at[pieces[chunk], LAGS - 1 + me], local_sem.at[chunk])
         copy.start()
-        own_copies.append(copy)
-
-    def keep_own(which):
-        copy = pltpu.make_async_copy(mixed.at[me, halves(which)], source.at[halves(which), LAGS - 1 + me], local_sem.at[which])
-        copy.start()
-        local_copies[which] = copy
-
-    def halo(to, which):
-        return remote(mixed.at[to, halves(which)], source.at[halves(which), jnp.maximum(me - 1, 0)], halo_send.at[0], halo_recv.at[which],
+        local_copies[chunk] = copy
+
+    def halo(to, chunk):
+        return remote(mixed.at[to, pieces[chunk]], source.at[pieces[chunk], jnp.maximum(me - 1, 0)], halo_send.at[0], halo_recv.at[chunk],
                       at(jnp.minimum(z + 1, last), to))
 
-    def forward(which):
-        return remote(source.at[halves(which), LAGS:LAGS + PLANE - 1], source.at[halves(which), 0:LAGS - 1], halo_send.at[1],
-                      halo_recv.at[which], at(jnp.minimum(z + 1, last), me))
+    def send_halo(chunk):
+        @pl.when((z < last) & (me > 0))
+        def _():
+            for to in places:
+                halo(to, chunk).start()
+
+    def forward(chunk):
+        return remote(source.at[pieces[chunk], LAGS:LAGS + PLANE - 1], source.at[pieces[chunk], 0:LAGS - 1], halo_send.at[1],
+                      halo_recv.at[chunk], at(jnp.minimum(z + 1, last), me))
+
+    landed = mixed.at[0:PLANE - 1, pl.ds(0, part)]
+
+    def wait_own(chunk):
+        local_copies[chunk].wait()
+        pltpu.make_async_copy(landed, landed, own_recv.at[chunk]).wait()
+
+    def send_forward(chunk):
+        wait_own(chunk)
+
+        @pl.when(z < last)
+        def _():
+            forward(chunk).start()
 
     places = [(me + step) % PLANE for step in range(1, PLANE)] + [me]
-    for which in ORDER:
-        for to in places:
-            mix(to, which)
-            if to is not me:
-                send_own(to, which)
-            if which in DIRECT:
-                @pl.when((z < last) & (me > 0))
-                def _(to=to, which=which):
-                    halo(to, which).start()
-        keep_own(which)
+
+    def run(stage):
+        for what, which in stage:
+            if what == "m":
+                for to in places:
+                    mix(to, which)
+            if what == "o":
+                send_own(which)
+            if what == "h":
+                send_halo(which)
+            if what == "f":
+                send_forward(which)
+
+    run(PLAN[0])
 
     loads[2].wait()
     pltpu.make_async_copy(taps_in.at[0:PLANE - 1], taps_in.at[0:PLANE - 1], tap_recv).wait()
@@ -137,6 +156,7 @@
             def _(step=step):
                 line(step).start()
     taps_all[z] = taps_own[...]
+    run(PLAN[1])
 
     loads[3].wait()
     per = BLOCK // GROUP
@@ -144,19 +164,7 @@
         row = skip_v[piece * BLOCK:(piece + 1) * BLOCK].reshape(1, BLOCK)
         skip_rows[piece * per:(piece + 1) * per] = jnp.broadcast_to(row, (BLOCK, BLOCK)).T.reshape(per, GROUP, BLOCK)
 
-    landed = mixed.at[0:PLANE - 1, pl.ds(0, half)]
-
-    def wait_own(which):
-        local_copies[which].wait()
-        pltpu.make_async_copy(landed, landed, own_recv.at[which]).wait()
-
-    for which in ORDER:
-        if which not in DIRECT:
-            wait_own(which)
-
-            @pl.when(z < last)
-            def _(which=which):
-                forward(which).start()
+    run(PLAN[2])
 
     @pl.when(z < last - 1)
     def _():
@@ -166,6 +174,8 @@
         @pl.when(z + step <= last)
         def _(step=step):
             line(step).start()
+
+    run(PLAN[3])
 
     u = lax.broadcasted_iota(jnp.int32, (BLOCK, BLOCK), 0)
     t = lax.broadcasted_iota(jnp.int32, (BLOCK, BLOCK), 1)
@@ -201,14 +211,12 @@
     back_copies = []
     for chunk in range(CHUNKS):
         rows = pl.ds(chunk * part, part)
-        which = chunk * part // half
-        if chunk * part % half == 0:
-            if which in DIRECT:
-                wait_own(which)
-
-            @pl.when(z > 0)
-            def _(which=which):
-                pltpu.make_async_copy(landed, landed, halo_recv.at[which]).wait()
+        if ("f", chunk) not in sum(PLAN, ()):
+            wait_own(chunk)
+
+        @pl.when(z > 0)
+        def _(chunk=chunk):
+            pltpu.make_async_copy(landed, landed, halo_recv.at[chunk]).wait()
 
         @pl.loop(chunk * part, (chunk + 1) * part, unroll=part)
         def _(g):
@@ -223,7 +231,7 @@
             copy = remote(result.at[to, rows], back.at[me, rows], back_send, back_recv, at(z, to))
             copy.start()
             back_copies.append(copy)
-    home = pltpu.make_async_copy(result.at[me], back.at[me], local_sem.at[2])
+    home = pltpu.make_async_copy(result.at[me], back.at[me], local_sem.at[CHUNKS])
     home.start()
     home.wait()
 
@@ -234,15 +242,16 @@
 
     @pl.when((z < last) & (me > 0))
     def _():
-        for which in DIRECT:
-            for _ in range(PLANE):
-                halo(me, which).wait_send()
+        for what, chunk in sum(PLAN, ()):
+            if what == "h":
+                for _ in range(PLANE):
+                    halo(me, chunk).wait_send()
 
     @pl.when(z < last)
     def _():
-        for which in range(2):
-            if which not in DIRECT:
-                forward(which).wait_send()
+        for what, chunk in sum(PLAN, ()):
+            if what == "f":
+                forward(chunk).wait_send()
 
     pltpu.make_async_copy(back.at[0:PLANE - 1], back.at[0:PLANE - 1], back_recv).wait()
 
@@ -282,10 +291,10 @@
                 pltpu.VMEM((planes, groups, BLOCK), f32),
                 pltpu.VMEM((groups, LAGS * BLOCK, BLOCK), bf16),
                 pltpu.VMEM((PLANE, groups, GROUP, BLOCK), bf16),
-                dma((4,)), dma((3,)),
+                dma((4,)), dma((CHUNKS + 1,)),
                 dma, dma, dma, dma((planes,)),
                 pltpu.SemaphoreType.REGULAR,
-                dma, dma((2,)), dma((2,)), dma((2,)), dma, dma,
+                dma, dma((CHUNKS,)), dma((2,)), dma((CHUNKS,)), dma, dma,
             ],
             compiler_params=pltpu.CompilerParams(collective_id=0, has_side_effects=True),
         )(key, value, filter_taps, skip)

time: 34.3 us -> 32.1 us (0.936)
  the two profiles are of different devices: /device:TPU:8 before, /device:TPU:192 now
where the time goes in v3:
time: 32.1 us; the launch traced here: 32 us
  Pallas kernels  32 us (100%)
    pallas_call x1, Pallas kernels, per_device(): pl.pallas_call(functools.partial(kernel, planes), out_shape=jax.ShapeDtyp...  29.9 us
    pallas_call x1, Pallas kernels, per_device(): pl.pallas_call(gate, grid=(steps,), out_shape=jax.ShapeDtypeStruct((token...  2.05 us

profile of v3, /device:TPU:192, one launch (start us, length us, event | category | flops | bytes accessed | tf_op | source)
XLA Modules:
  0.0 32.0 jit_solution(6276120369232518090)
XLA Ops:
  0.0 29.9 %shard_map.55 = bf16[8,16,16,128]{3,2,1,0:T(8,128)(2,1)} custom-call(bf16[128,2048]{1,0:T(8,128)(2,1)} %k_hbm.1, bf16[128,2048]{1,0:T(8,128)(2,1)} %v_hbm.1, bf16[16,128]{1,0:T(8,128)(2,1)} %taps_hbm.1, f32[2048]{0:T(1024)} %skip_hbm.1), custom_call_target="tpu_custom_call" | custom-call | tf_op jit(solution)/shard_map/pallas_call | solution.py:275
  29.9 2.0 %shard_map.56 = bf16[128,2048]{1,0:T(8,128)(2,1)} custom-call(bf16[2048,128]{1,0:T(8,128)(2,1)} %bitcast.1, bf16[128,2048]{1,0:T(8,128)(2,1)} %q_ref.1), custom_call_target="tpu_custom_call" | custom-call | tf_op jit(solution)/shard_map/pallas_call | solution.py:302

commit v4 on v3

--- a/solution.py
+++ b/solution.py
@@ -158,6 +158,15 @@
     taps_all[z] = taps_own[...]
     run(PLAN[1])
 
+    @pl.when(z < last - 1)
+    def _():
+        pl.semaphore_wait(credit, last - 1 - z)
+
+    for step in range(2, planes):
+        @pl.when(z + step <= last)
+        def _(step=step):
+            line(step).start()
+
     loads[3].wait()
     per = BLOCK // GROUP
     for piece in range(groups // per):
@@ -166,14 +175,6 @@
 
     run(PLAN[2])
 
-    @pl.when(z < last - 1)
-    def _():
-        pl.semaphore_wait(credit, last - 1 - z)
-
-    for step in range(2, planes):
-        @pl.when(z + step <= last)
-        def _(step=step):
-            line(step).start()
 
     run(PLAN[3])
 

time: 32.1 us -> 30.8 us (0.960)
  the two profiles are of different devices: /device:TPU:192 before, /device:TPU:8 now
where the time goes in v4:
time: 30.8 us; the launch traced here: 30.7 us
  Pallas kernels  30.7 us (100%)
    pallas_call x1, Pallas kernels, per_device(): pl.pallas_call(functools.partial(kernel, planes), out_shape=jax.ShapeDtyp...  28.6 us
    pallas_call x1, Pallas kernels, per_device(): pl.pallas_call(gate, grid=(steps,), out_shape=jax.ShapeDtypeStruct((token...  2.05 us

profile of v4, /device:TPU:8, one launch (start us, length us, event | category | flops | bytes accessed | tf_op | source)
XLA Modules:
  0.0 30.7 jit_solution(11865448297922685541)
XLA Ops:
  0.0 28.6 %shard_map.55 = bf16[8,16,16,128]{3,2,1,0:T(8,128)(2,1)} custom-call(bf16[128,2048]{1,0:T(8,128)(2,1)} %k_hbm.1, bf16[128,2048]{1,0:T(8,128)(2,1)} %v_hbm.1, bf16[16,128]{1,0:T(8,128)(2,1)} %taps_hbm.1, f32[2048]{0:T(1024)} %skip_hbm.1), custom_call_target="tpu_custom_call" | custom-call | tf_op jit(solution)/shard_map/pallas_call | solution.py:276
  28.6 2.0 %shard_map.56 = bf16[128,2048]{1,0:T(8,128)(2,1)} custom-call(bf16[2048,128]{1,0:T(8,128)(2,1)} %bitcast.1, bf16[128,2048]{1,0:T(8,128)(2,1)} %q_ref.1), custom_call_target="tpu_custom_call" | custom-call | tf_op jit(solution)/shard_map/pallas_call | solution.py:303

commit v5 on v4

--- a/solution.py
+++ b/solution.py
@@ -12,7 +12,7 @@
 BLOCK = 128
 LAGS = 8
 PLANE = 8
-PLAN = ((('m', 0), ('m', 1), ('o', 3), ('o', 0), ('h', 0), ('h', 1)), (('h', 2), ('o', 1), ('o', 2)), (('f', 3),), ())
+PLAN = ((('m', 0), ('m', 1), ('o', 2), ('h', 0), ('o', 3), ('x', 1)), (('y', 1), ('o', 0), ('o', 1)), (('f', 2), ('f', 3)), ())
 STEPS = 2
 CHUNKS = 4
 
@@ -139,6 +139,10 @@
                 send_halo(which)
             if what == "f":
                 send_forward(which)
+            if what in "xy":
+                @pl.when(ch % 2 == (0 if what == "x" else 1))
+                def _(which=which):
+                    send_halo(which)
 
     run(PLAN[0])
 
@@ -244,7 +248,7 @@
     @pl.when((z < last) & (me > 0))
     def _():
         for what, chunk in sum(PLAN, ()):
-            if what == "h":
+            if what in "hx":
                 for _ in range(PLANE):
                     halo(me, chunk).wait_send()
 

time: 30.8 us -> 30.2 us (0.981)
  Pallas kernels: 30.7 us -> 30.1 us
    pallas_call x1, Pallas kernels: 28.6 us -> 28.1 us  [per_device(): pl.pallas_call(functools.partial(kernel, planes), out_shape=jax.ShapeDtyp...]
where the time goes in v5:
time: 30.2 us; the launch traced here: 30.1 us
  Pallas kernels  30.1 us (100%)
    pallas_call x1, Pallas kernels, per_device(): pl.pallas_call(functools.partial(kernel, planes), out_shape=jax.ShapeDtyp...  28.1 us
    pallas_call x1, Pallas kernels, per_device(): pl.pallas_call(gate, grid=(steps,), out_shape=jax.ShapeDtypeStruct((token...  2.05 us

profile of v5, /device:TPU:8, one launch (start us, length us, event | category | flops | bytes accessed | tf_op | source)
XLA Modules:
  0.0 30.1 jit_solution(5613745033867349159)
XLA Ops:
  0.0 28.1 %shard_map.55 = bf16[8,16,16,128]{3,2,1,0:T(8,128)(2,1)} custom-call(bf16[128,2048]{1,0:T(8,128)(2,1)} %k_hbm.1, bf16[128,2048]{1,0:T(8,128)(2,1)} %v_hbm.1, bf16[16,128]{1,0:T(8,128)(2,1)} %taps_hbm.1, f32[2048]{0:T(1024)} %skip_hbm.1), custom_call_target="tpu_custom_call" | custom-call | tf_op jit(solution)/shard_map/pallas_call | solution.py:280
  28.1 2.0 %shard_map.56 = bf16[128,2048]{1,0:T(8,128)(2,1)} custom-call(bf16[2048,128]{1,0:T(8,128)(2,1)} %bitcast.1, bf16[128,2048]{1,0:T(8,128)(2,1)} %q_ref.1), custom_call_target="tpu_custom_call" | custom-call | tf_op jit(solution)/shard_map/pallas_call | solution.py:307

commit v6 on v5

--- a/solution.py
+++ b/solution.py
@@ -12,7 +12,7 @@
 BLOCK = 128
 LAGS = 8
 PLANE = 8
-PLAN = ((('m', 0), ('m', 1), ('o', 2), ('h', 0), ('o', 3), ('x', 1)), (('y', 1), ('o', 0), ('o', 1)), (('f', 2), ('f', 3)), ())
+PLAN = ((('m', 0), ('m', 1), ('o', 2), ('h', 0), ('o', 3), ('x', 1)), (('o', 0), ('y', 1), ('o', 1)), (('f', 2), ('f', 3)), ())
 STEPS = 2
 CHUNKS = 4
 

time: 30.2 us -> 30.2 us (level)
  no operation moved by 1% of the time
where the time goes in v6:
time: 30.2 us; the launch traced here: 30.1 us
  Pallas kernels  30.1 us (100%)
    pallas_call x1, Pallas kernels, per_device(): pl.pallas_call(functools.partial(kernel, planes), out_shape=jax.ShapeDtyp...  28.1 us
    pallas_call x1, Pallas kernels, per_device(): pl.pallas_call(gate, grid=(steps,), out_shape=jax.ShapeDtypeStruct((token...  2.05 us

profile of v6, /device:TPU:8, one launch (start us, length us, event | category | flops | bytes accessed | tf_op | source)
XLA Modules:
  0.0 30.1 jit_solution(4862586526687909300)
XLA Ops:
  0.0 28.1 %shard_map.55 = bf16[8,16,16,128]{3,2,1,0:T(8,128)(2,1)} custom-call(bf16[128,2048]{1,0:T(8,128)(2,1)} %k_hbm.1, bf16[128,2048]{1,0:T(8,128)(2,1)} %v_hbm.1, bf16[16,128]{1,0:T(8,128)(2,1)} %taps_hbm.1, f32[2048]{0:T(1024)} %skip_hbm.1), custom_call_target="tpu_custom_call" | custom-call | tf_op jit(solution)/shard_map/pallas_call | solution.py:280
  28.1 2.0 %shard_map.56 = bf16[128,2048]{1,0:T(8,128)(2,1)} custom-call(bf16[2048,128]{1,0:T(8,128)(2,1)} %bitcast.1, bf16[128,2048]{1,0:T(8,128)(2,1)} %q_ref.1), custom_call_target="tpu_custom_call" | custom-call | tf_op jit(solution)/shard_map/pallas_call | solution.py:307

commit v7 on v6

--- a/solution.py
+++ b/solution.py
@@ -12,7 +12,7 @@
 BLOCK = 128
 LAGS = 8
 PLANE = 8
-PLAN = ((('m', 0), ('m', 1), ('o', 2), ('h', 0), ('o', 3), ('x', 1)), (('o', 0), ('y', 1), ('o', 1)), (('f', 2), ('f', 3)), ())
+PLAN = ((('m', 1), ('o', 2), ('m', 0), ('h', 0), ('o', 3), ('x', 1)), (('o', 0), ('y', 1), ('o', 1)), (('f', 2), ('f', 3)), ())
 STEPS = 2
 CHUNKS = 4
 

time: 30.2 us -> 30.5 us (level); the launches traced: 30.1 us -> 30.1 us
  no operation moved by 1% of the time
where the time goes in v7:
time: 30.5 us; the launch traced here: 30.1 us
  Pallas kernels  30.1 us (99%)
    pallas_call x1, Pallas kernels, per_device(): pl.pallas_call(functools.partial(kernel, planes), out_shape=jax.ShapeDtyp...  28 us
    pallas_call x1, Pallas kernels, per_device(): pl.pallas_call(gate, grid=(steps,), out_shape=jax.ShapeDtypeStruct((token...  2.05 us

profile of v7, /device:TPU:8, one launch (start us, length us, event | category | flops | bytes accessed | tf_op | source)
XLA Modules:
  0.0 30.1 jit_solution(5486627254006814400)
XLA Ops:
  0.0 28.0 %shard_map.55 = bf16[8,16,16,128]{3,2,1,0:T(8,128)(2,1)} custom-call(bf16[128,2048]{1,0:T(8,128)(2,1)} %k_hbm.1, bf16[128,2048]{1,0:T(8,128)(2,1)} %v_hbm.1, bf16[16,128]{1,0:T(8,128)(2,1)} %taps_hbm.1, f32[2048]{0:T(1024)} %skip_hbm.1), custom_call_target="tpu_custom_call" | custom-call | tf_op jit(solution)/shard_map/pallas_call | solution.py:280
  28.0 2.0 %shard_map.56 = bf16[128,2048]{1,0:T(8,128)(2,1)} custom-call(bf16[2048,128]{1,0:T(8,128)(2,1)} %bitcast.1, bf16[128,2048]{1,0:T(8,128)(2,1)} %q_ref.1), custom_call_target="tpu_custom_call" | custom-call | tf_op jit(solution)/shard_map/pallas_call | solution.py:307
